TPU v7x, 32 devices: a whole 2x2x4 slice. The times are simulated.
32 devices in a mesh: row: 8 (over z, x), col: 4 (over y, core).
Axes of the slice: x: 2, y: 2, z: 4, core: 2. Of those that a mesh axis runs over, the one named last changes fastest.
Arguments:
- geneo_vectors: bfloat16 [32, 32, 512, 512], P(None, None, 'row', 'col'), as said below
- phase_labels: int32 [32, 512, 512], P(None, 'row', 'col'), may hold values from 0 to 3, as said below
- phase_mobility: float32 [4], replicated, may hold values from 0.5 to 5
Outputs:
- coarse_factor: float32 [32, 4, 4, 2, 2, 8, 2, 32], P(None, None, 'col', None, None, 'row')
Inputs may be any that keep to these rules, and one draw needn't show every extreme that they name: `geneo_vectors`: the 32 vectors of each subdomain are linearly independent on its cells. `phase_labels`: within one subdomain the labels take one or two values, some q and (q + 1) modulo 4.
All inputs are finite; a program needn't handle non-finite values.
Results may differ from a plain program's by a relative error of at most 0.00055.
Values may be sent and summed in bfloat16 or wider, within the bound.
A program may use at most 512 MiB of HBM per device.

v0:
```python
import jax
import jax.numpy as jnp
from jax import lax
from jax.sharding import PartitionSpec as P

NB = 2
PSUB = 2
FACES = ((-1, 0), (1, 0), (0, -1), (0, 1))


def with_halo(cells, sides, width):
    for axis, dim in sides:
        count = lax.axis_size(axis)
        ends = count - 1
        head = lax.slice_in_dim(cells, 0, width, axis=dim)
        tail = lax.slice_in_dim(cells, cells.shape[dim] - width, cells.shape[dim], axis=dim)
        cells = jnp.concatenate(
            [
                lax.ppermute(tail, axis, [(i, (i + 1) % count) for i in range(ends)]),
                cells,
                lax.ppermute(head, axis, [((i + 1) % count, i) for i in range(ends)]),
            ],
            axis=dim,
        )
    return cells


def slot_offsets():
    offsets = [((0, 0), (0, 0))]
    for face in FACES:
        offsets += [((0, 0), face), (face, (0, 0)), (face, face)]
    for face_x in FACES[:2]:
        for face_y in FACES[2:]:
            offsets += [(face_x, face_y), (face_y, face_x)]
    return offsets


def band_index(from_off, to_off):
    return (to_off[0] - from_off[0] + 1) * 3 + (to_off[1] - from_off[1] + 1)


def from_next(field, axis):
    count = field.shape[axis]
    inner = lax.slice_in_dim(field, 1, count, axis=axis)
    blank = jnp.zeros_like(lax.slice_in_dim(field, 0, 1, axis=axis))
    return jnp.concatenate([inner, blank], axis=axis)


def from_prev(field, axis):
    count = field.shape[axis]
    inner = lax.slice_in_dim(field, 0, count - 1, axis=axis)
    blank = jnp.zeros_like(lax.slice_in_dim(field, 0, 1, axis=axis))
    return jnp.concatenate([blank, inner], axis=axis)


def laplace_own(own):
    field = own.astype(jnp.float32)
    near = from_next(field, 1) + from_prev(field, 1)
    near = near + from_next(field, 2) + from_prev(field, 2)
    near = near + from_next(field, 3) + from_prev(field, 3)
    return near - 6.0 * field


def contract_cells(left, right):
    flat_left = left.reshape(left.shape[0], -1)
    flat_right = right.reshape(right.shape[0], -1)
    return lax.dot_general(
        flat_left, flat_right, (((1,), (1,)), ((), ())), preferred_element_type=jnp.float32
    )


def local_tiles(own, labels, mobility_table):
    rims_x = jnp.stack([own[:, :, 0, :], own[:, :, -1, :]], axis=2)
    wide_x = with_halo(rims_x, (("row", 2),), 1)
    rims_y = jnp.stack([own[:, :, :, 0], own[:, :, :, -1]], axis=2)
    wide_y = with_halo(rims_y, (("col", 2),), 1)
    lower_x = wide_x[:, :, 0, :]
    upper_x = wide_x[:, :, 3, :]
    lower_y = wide_y[:, :, 0, :]
    upper_y = wide_y[:, :, 3, :]
    root_table = jnp.sqrt(mobility_table)
    cell_root = jnp.zeros(labels.shape, jnp.float32)
    for phase in range(mobility_table.shape[0]):
        cell_root = cell_root + jnp.where(labels == phase, root_table[phase], jnp.float32(0.0))
    flux = (laplace_own(own) * cell_root).astype(jnp.bfloat16)
    tiles = [contract_cells(own, own) + contract_cells(flux, flux)]
    face_data = [
        (flux[:, :, 0, :], lower_x, cell_root[:, 0, :]),
        (flux[:, :, -1, :], upper_x, cell_root[:, -1, :]),
        (flux[:, :, :, 0], lower_y, cell_root[:, :, 0]),
        (flux[:, :, :, -1], upper_y, cell_root[:, :, -1]),
    ]
    for layer_f, layer_z, layer_r in face_data:
        across = (layer_z.astype(jnp.float32) * layer_r).astype(jnp.bfloat16)
        cross = contract_cells(layer_f, across)
        tiles += [cross, cross.T, contract_cells(across, across)]
    for x_first in (True, False):
        for y_first in (True, False):
            layer_x = lower_x if x_first else upper_x
            layer_y = lower_y if y_first else upper_y
            cell_x = 0 if x_first else -1
            cell_y = 0 if y_first else -1
            corner_r = cell_root[:, cell_x, cell_y]
            along_x = (layer_x[:, :, cell_y].astype(jnp.float32) * corner_r).astype(jnp.bfloat16)
            along_y = (layer_y[:, :, cell_x].astype(jnp.float32) * corner_r).astype(jnp.bfloat16)
            pair = contract_cells(along_x, along_y)
            tiles += [pair, pair.T]
    return jnp.stack(tiles)


def shift_grid(values, offset):
    widths = [(1, 1), (1, 1)] + [(0, 0)] * (values.ndim - 2)
    padded = jnp.pad(values, widths)
    start_x = 1 - offset[0]
    start_y = 1 - offset[1]
    return padded[start_x : start_x + values.shape[0], start_y : start_y + values.shape[1]]


def to_owner(stack, n_row, n_col):
    slots = stack.shape[0]
    vectors = stack.shape[1]
    row_blocks = vectors // (NB * n_row)
    col_blocks = vectors // (NB * n_col)
    split = stack.reshape(slots, row_blocks, n_row, NB, col_blocks, n_col, NB)
    moved = split.transpose(2, 5, 0, 4, 6, 1, 3)
    return moved.reshape(n_row, n_col, slots * col_blocks * NB * row_blocks * NB)


def place_bands(bands, n_row, n_col):
    n_sub = n_row * n_col
    sub_x = jnp.arange(n_sub, dtype=jnp.int32) // n_col
    sub_y = jnp.arange(n_sub, dtype=jnp.int32) % n_col
    total = None
    for index in range(9):
        step_x = index // 3 - 1
        step_y = index % 3 - 1
        match = (
            (sub_x[:, None] == sub_x[None, :] + step_x)
            & (sub_y[:, None] == sub_y[None, :] + step_y)
        ).astype(jnp.float32)
        flat = bands[index].reshape(n_sub, -1).T
        term = match[:, None, :] * flat[None, :, :]
        total = term if total is None else total + term
    return total


def body(geneo_vectors, phase_labels, phase_mobility):
    vectors = geneo_vectors.shape[0]
    n_row = lax.axis_size("row")
    n_col = lax.axis_size("col")
    n_sub = n_row * n_col
    row_blocks = vectors // (NB * n_row)
    col_blocks = vectors // (NB * n_col)
    rows_here = row_blocks * NB * n_sub
    piece_len = col_blocks * NB * row_blocks * NB
    width = PSUB * vectors
    tiles = local_tiles(geneo_vectors, phase_labels, phase_mobility)
    offsets = slot_offsets()
    routed = lax.all_to_all(
        lax.all_to_all(
            to_owner(tiles, n_row, n_col), "row", split_axis=0, concat_axis=0, tiled=True
        ),
        "col",
        split_axis=1,
        concat_axis=1,
        tiled=True,
    )
    routed = routed.reshape(n_row, n_col, len(offsets), piece_len)
    bands = [jnp.zeros((n_row, n_col, piece_len), jnp.float32) for count in range(9)]
    for slot, pair_off in enumerate(offsets):
        place = band_index(pair_off[0], pair_off[1])
        bands[place] = bands[place] + shift_grid(routed[:, :, slot], pair_off[0])
    local = place_bands(bands, n_row, n_col).reshape(n_sub, col_blocks * NB, rows_here)
    col_index = lax.axis_index("col")
    row_sub = jnp.arange(rows_here, dtype=jnp.int32) % n_sub
    col_sub = jnp.arange(n_sub, dtype=jnp.int32)
    for panel in range(2):
        first = panel * PSUB
        last = first + PSUB
        part = local[first:last].reshape(PSUB, col_blocks, 1, NB, rows_here)
        whole = lax.all_gather(part, "col", axis=2, tiled=True).reshape(width, rows_here)
        diag_part = whole.reshape(width, row_blocks, 1, NB, n_sub)[:, :, :, :, first:last]
        diag_all = lax.all_gather(diag_part, "row", axis=2, tiled=True)
        diag = diag_all.transpose(0, 4, 1, 2, 3).reshape(width, width).T
        low = jnp.linalg.cholesky(diag)
        solved = lax.linalg.triangular_solve(low, whole, left_side=True, lower=True)
        solved = jnp.where(row_sub[None, :] >= first, solved, jnp.float32(0.0))
        mine = lax.dynamic_index_in_dim(
            solved.reshape(PSUB, col_blocks, n_col, NB, rows_here), col_index, 2, keepdims=False
        )
        local = local.at[first:last].set(mine.reshape(PSUB, col_blocks * NB, rows_here))
        gathered = lax.all_gather(
            solved.reshape(width, row_blocks, 1, NB, n_sub).astype(jnp.bfloat16),
            "row",
            axis=2,
            tiled=True,
        ).astype(jnp.float32)
        picked = lax.dynamic_index_in_dim(
            gathered.reshape(width, row_blocks, n_row // n_col, n_col, NB, n_sub),
            col_index,
            3,
            keepdims=False,
        )
        columns = (
            picked.reshape(width, col_blocks, NB, n_sub)
            .transpose(0, 3, 1, 2)
            .reshape(width, n_sub * col_blocks * NB)
        )
        update = lax.dot_general(
            columns,
            solved,
            (((0,), (0,)), ((), ())),
            precision=lax.Precision.HIGHEST,
            preferred_element_type=jnp.float32,
        )
        update = update.reshape(n_sub, col_blocks * NB, rows_here)
        trailing = (col_sub >= last)[:, None, None]
        above = (row_sub < last)[None, None, :]
        local = jnp.where(trailing, jnp.where(above, jnp.float32(0.0), local - update), local)
    return local.reshape(n_sub, col_blocks, 1, NB, row_blocks, 1, NB, n_sub)


def solution(mesh):
    return jax.shard_map(
        body,
        mesh=mesh,
        in_specs=(P(None, None, "row", "col"), P(None, "row", "col"), P()),
        out_specs=P(None, None, "col", None, None, "row", None, None),
        check_vma=False,
    )
```

profile of v0, /device:TPU:0, one launch (start us, length us, event | category | flops | bytes accessed | tf_op | source)
XLA Modules:
  0.0 737.6 jit_solution(1888599617356064845)
XLA Ops:
  0.0 25.4 %fusion.90 = (bf16[32,32,64,1]{3,2,1,0:T(8,128)(2,1)}, bf16[32,32,64,1]{3,2,1,0:T(8,128)(2,1)}) fusion(bf16[32,32,64,128]{3,2,1,0:T(8,128)(2,1)} %param.10), kind=kLoop, calls=%fused_computation.168 | loop fusion | bytes 524288 | tf_op jit(solution)/shard_map/slice | solution.py:75
  25.4 19.4 %copy.541 = bf16[32,32,64,1]{1,0,2,3:T(8,128)(2,1)} copy(bf16[32,32,64,1]{3,2,1,0:T(8,128)(2,1)} %get-tuple-element.42) | data formatting | bytes 262144
  44.8 3.2 collective-permute-start.2
  48.0 19.4 %copy.542 = bf16[32,32,64,1]{1,0,2,3:T(8,128)(2,1)} copy(bf16[32,32,64,1]{3,2,1,0:T(8,128)(2,1)} %get-tuple-element.41) | data formatting | bytes 262144
  68.6 3.4 fusion.92
  74.8 5.5 collective-permute-start
  80.3 21.9 %copy_convert_fusion = f32[32,32,64,128]{3,0,1,2:T(8,128)} fusion(bf16[32,32,64,128]{3,2,1,0:T(8,128)(2,1)} %param.10), kind=kLoop, calls=%fused_computation.3 | loop fusion | flops 8388608 | bytes 50331648 | tf_op jit(solution)/shard_map/convert_element_type | solution.py:57
  102.2 45.9 %fusion.89 = (f32[32,32,64,127]{3,0,1,2:T(8,128)}, f32[32,32,64,127]{3,0,1,2:T(8,128)}) fusion(f32[32,32,64,128]{3,0,1,2:T(8,128)} %copy_convert_fusion), kind=kLoop, calls=%fused_computation.167 | loop fusion | bytes 133169152 | tf_op jit(solution)/shard_map/slice | solution.py:44
  148.1 44.0 %fusion.88 = (f32[32,32,63,128]{3,0,1,2:T(8,128)}, f32[32,32,63,128]{3,0,1,2:T(8,128)}) fusion(f32[32,32,64,128]{3,0,1,2:T(8,128)} %copy_convert_fusion), kind=kLoop, calls=%fused_computation.166 | loop fusion | bytes 132120576 | tf_op jit(solution)/shard_map/slice | solution.py:44
  192.1 41.5 %fusion.87 = (f32[32,31,64,128]{3,0,1,2:T(8,128)}, f32[32,31,64,128]{3,0,1,2:T(8,128)}) fusion(f32[32,32,64,128]{3,0,1,2:T(8,128)} %copy_convert_fusion), kind=kLoop, calls=%fused_computation.165 | loop fusion | bytes 130023424 | tf_op jit(solution)/shard_map/slice | solution.py:44
  234.2 3.3 select_add_fusion
  238.5 34.2 %fusion.8 = f32[32,32]{1,0:T(8,128)S(1)} fusion(bf16[32,32,64,128]{3,2,1,0:T(8,128)(2,1)} %param.10), kind=kOutput, calls=%fused_computation.18 | convolution fusion | flops 536870912 | bytes 16781312 | tf_op jit(solution)/shard_map/dot_general | solution.py:67
  273.4 71.5 %multiply_convert_fusion = bf16[32,32,64,128]{3,0,1,2:T(8,128)(2,1)} fusion(f32[32,32,64,127]{3,0,1,2:T(8,128)} %get-tuple-element.40, f32[32,32,64,127]{3,0,1,2:T(8,128)} %get-tuple-element.39, f32[32,32,63,128]{3,0,1,2:T(8,128)} %get-tuple-element.38, f32[32,32,63,128]{3,0,1,2:T(8,128)} %get-tuple-element.37, f32[32,31,64,128]{3,0,1,2:T(8,128)} %get-tuple-element.36, ...), kind=kLoop, calls=%fused_computation | loop fusion | flops 83886080 | bytes 232259584 | tf_op jit(solution)/shard_map/convert_element_type | solution.py:85
  344.9 25.9 %fusion.91 = (bf16[32,32,64,1]{3,0,1,2:T(8,128)(2,1)}, bf16[32,32,64,1]{3,0,1,2:T(8,128)(2,1)}) fusion(bf16[32,32,64,128]{3,0,1,2:T(8,128)(2,1)} %multiply_convert_fusion), kind=kLoop, calls=%fused_computation.169 | loop fusion | bytes 524288 | tf_op jit(solution)/shard_map/slice | solution.py:91
  370.8 13.5 %fusion.14 = f32[32,32]{1,0:T(8,128)} fusion(f32[32,32]{1,0:T(8,128)S(1)} %fusion.8, bf16[32,32,64,128]{3,0,1,2:T(8,128)(2,1)} %multiply_convert_fusion), kind=kOutput, calls=%fused_computation.20 | convolution fusion | flops 536871936 | bytes 16785408 | tf_op jit(solution)/shard_map/dot_general | solution.py:67
  385.6 21.2 %copy.385 = bf16[32,32,64,1]{2,1,0,3:T(8,128)(2,1)S(1)} copy(bf16[32,32,64,1]{3,0,1,2:T(8,128)(2,1)} %get-tuple-element.44) | data formatting | bytes 262144 | tf_op jit(solution)/shard_map/slice | solution.py:90
  407.5 21.4 %copy.393 = bf16[32,32,64,1]{2,1,0,3:T(8,128)(2,1)S(1)} copy(bf16[32,32,64,1]{3,0,1,2:T(8,128)(2,1)} %get-tuple-element.43) | data formatting | bytes 262144 | tf_op jit(solution)/shard_map/slice | solution.py:91
  430.7 3.1 copy.408
  441.6 3.1 copy.415
  444.9 3.4 copy.416
  451.9 3.4 copy.419
  464.4 3.9 copy.412
  468.5 4.2 copy.413
  475.2 3.9 copy.409
  479.3 4.2 copy.410
  490.5 3.2 copy.401
  494.9 3.9 copy.421
  499.0 4.2 copy.422
  504.3 4.0 copy.423
  508.5 4.1 copy.424
  516.0 3.9 copy.425
  520.1 4.1 copy.426
  526.6 3.9 copy.427
  530.7 4.2 copy.428
  534.9 7.7 %stack.75 = f32[21,2,8,2,4,4,2]{0,2,6,5,4,3,1:T(8,128)} concatenate(f32[1,2,8,2,4,4,2]{0,2,6,5,4,3,1:T(8,128)S(1)} %copy.408, f32[1,2,8,2,4,4,2]{0,2,6,5,4,3,1:T(8,128)} %copy.409, f32[1,2,8,2,4,4,2]{0,2,6,5,4,3,1:T(8,128)} %copy.410, f32[1,2,8,2,4,4,2]{0,2,6,5,4,3,1:T(8,128)} %copy.411, f32[1,2,8,2,4,4,2]{0,2,6,5,4,3,1:T(8,128)} %copy.412, f32[1,2,8,2,4,4,2]{0,2,6,5,4,3,1:T(8,128)} %copy.413, ...), dimensions={0} | concatenate | bytes 172032 | tf_op jit(solution)/shard_map/stack | solution.py:108
  546.5 5.5 all-to-all-start
  563.8 4.5 all-to-all-start.1
  568.3 4.3 all-to-all-done.1
  575.7 5.2 all_gather.18
  581.1 31.4 %all_gather.19 = f32[64,2,8,2,2]{0,4,3,1,2:T(2,128)S(1)} all-gather(f32[64,2,1,2,2]{0,4,3,1,2:T(2,128)S(1)} %copy.471), channel_id=1, replica_groups=mesh['row'=8,'col'=4] {'row'}, dimensions={2}, use_global_device_ids=true | all-gather | bytes 18432 | tf_op jit(solution)/shard_map/all_gather | solution.py:183
  612.6 5.8 cholesky.44
  619.8 4.9 custom-call.6
  625.0 30.7 %all_gather.20 = bf16[64,2,8,2,32]{0,4,3,1,2:T(8,128)(2,1)S(1)} all-gather(bf16[64,2,1,2,32]{0,4,3,1,2:T(8,128)(2,1)S(1)} %bitcast.334), channel_id=1, replica_groups=mesh['row'=8,'col'=4] {'row'}, dimensions={2}, use_global_device_ids=true | all-gather | bytes 147456 | tf_op jit(solution)/shard_map/all_gather | solution.py:192
  656.2 5.2 all_gather.21
  661.8 30.6 %all_gather.22 = f32[64,2,8,2,2]{0,4,3,1,2:T(2,128)S(1)} all-gather(f32[64,2,1,2,2]{0,4,3,1,2:T(2,128)S(1)} %copy.479), channel_id=1, replica_groups=mesh['row'=8,'col'=4] {'row'}, dimensions={2}, use_global_device_ids=true | all-gather | bytes 18432 | tf_op jit(solution)/shard_map/all_gather | solution.py:183
  692.6 5.8 cholesky.55
  699.8 4.9 custom-call.7
  705.0 30.7 %all_gather.23 = bf16[64,2,8,2,32]{0,4,3,1,2:T(8,128)(2,1)S(1)} all-gather(bf16[64,2,1,2,32]{0,4,3,1,2:T(8,128)(2,1)S(1)} %bitcast.335), channel_id=1, replica_groups=mesh['row'=8,'col'=4] {'row'}, dimensions={2}, use_global_device_ids=true | all-gather | bytes 147456 | tf_op jit(solution)/shard_map/all_gather | solution.py:192
  (193 shorter events, 73.9 us)
Async XLA Ops:
  44.8 389.9 %collective-permute-start.2 = (bf16[32,32,1,64]{1,0,3,2:T(8,128)(2,1)}, bf16[32,32,1,64]{1,0,3,2:T(8,128)(2,1)}, u32[]{:S(2)}, u32[]{:S(2)}) collective-permute-start(bf16[32,32,1,64]{1,0,3,2:T(8,128)(2,1)} %bitcast.32), channel_id=1, source_target_pairs={{0,1},{1,2},{2,3},{4,5},{5,6},{6,7},{8,9},{9,10},{10,11},{12,13},{... | collective-permute-start | bytes 393224 | tf_op jit(solution)/shard_map/ppermute | solution.py:19
  67.3 369.4 %collective-permute-start.3 = (bf16[32,32,1,64]{1,0,3,2:T(8,128)(2,1)}, bf16[32,32,1,64]{1,0,3,2:T(8,128)(2,1)}, u32[]{:S(2)}, u32[]{:S(2)}) collective-permute-start(bf16[32,32,1,64]{1,0,3,2:T(8,128)(2,1)} %bitcast.43), channel_id=1, source_target_pairs={{1,0},{2,1},{3,2},{5,4},{6,5},{7,6},{9,8},{10,9},{11,10},{13,12},{... | collective-permute-start | bytes 393224 | tf_op jit(solution)/shard_map/ppermute | solution.py:21
  72.7 389.1 %collective-permute-start.1 = (bf16[32,32,1,128]{3,1,0,2:T(8,128)(2,1)}, bf16[32,32,1,128]{3,1,0,2:T(8,128)(2,1)}, u32[]{:S(2)}, u32[]{:S(2)}) collective-permute-start(bf16[32,32,1,128]{3,1,0,2:T(8,128)(2,1)} %copy.540), channel_id=1, source_target_pairs={{4,0},{8,4},{12,8},{16,12},{20,16},{24,20},{28,24},{5,1},{9,5},{13... | collective-permute-start | bytes 786440 | tf_op jit(solution)/shard_map/ppermute | solution.py:21
  74.8 397.9 %collective-permute-start = (bf16[32,32,1,128]{3,1,2,0:T(8,128)(2,1)}, bf16[32,32,1,128]{3,1,2,0:T(8,128)(2,1)}, u32[]{:S(2)}, u32[]{:S(2)}) collective-permute-start(bf16[32,32,1,128]{3,1,2,0:T(8,128)(2,1)} %copy.539), channel_id=1, source_target_pairs={{0,4},{4,8},{8,12},{12,16},{16,20},{20,24},{24,28},{1,5},{5,9},{9,... | collective-permute-start | bytes 786440 | tf_op jit(solution)/shard_map/ppermute | solution.py:19
  192.1 41.5 %copy-start.4 = (f32[4]{0:T(128)S(1)}, f32[4]{0:T(128)}, u32[]{:S(2)}) copy-start(f32[4]{0:T(128)} %param.12) | copy-start | bytes 52
  192.1 42.2 %copy-start = (s32[32,64,128]{2,1,0:T(8,128)S(1)}, s32[32,64,128]{2,1,0:T(8,128)}, u32[]{:S(2)}) copy-start(s32[32,64,128]{2,1,0:T(8,128)} %param.11) | copy-start | bytes 3145732
  440.2 85.3 %copy-start.1 = (f32[32]{0:T(128)S(1)}, f32[32]{0:T(128)}, u32[]{:S(2)}) copy-start(f32[32]{0:T(128)} %get-tuple-element.31) | copy-start | bytes 388
  441.1 183.6 %copy-start.3 = (pred[128]{0:T(512)(128)(4,1)S(1)}, pred[128]{0:T(512)(128)(4,1)}, u32[]{:S(2)}) copy-start(pred[128]{0:T(512)(128)(4,1)} %broadcast_compare_fusion.3) | copy-start | bytes 388
  448.3 207.7 %copy-start.2 = (pred[32]{0:T(512)(128)(4,1)S(1)}, pred[32]{0:T(512)(128)(4,1)}, u32[]{:S(2)}) copy-start(pred[32]{0:T(512)(128)(4,1)} %iota_compare_fusion.2) | copy-start | bytes 100
  546.5 16.6 %all-to-all-start = ((f32[8,4,672]{2,1,0:T(4,128)}), f32[8,4,672]{2,1,0:T(4,128)S(1)}, u32[]{:S(2)}, u32[]{:S(2)}) async-start(f32[8,4,672]{2,1,0:T(4,128)} %copy.430), calls=%async_computation | async-start | bytes 196608 | tf_op jit(solution)/shard_map/all_to_all | solution.py:160
  563.8 8.8 %all-to-all-start.1 = ((f32[8,4,672]{2,0,1:T(8,128)}), f32[8,4,672]{2,0,1:T(8,128)S(1)}, u32[]{:S(2)}, u32[]{:S(2)}) async-start(f32[8,4,672]{2,0,1:T(8,128)} %copy.431), calls=%async_computation.1 | async-start | bytes 196608 | tf_op jit(solution)/shard_map/all_to_all | solution.py:159
where the time goes:
time: 749 us; the launch traced here: 738 us
  local copies, waits for them, and re-layouts  388 us (52%)
  blocking collectives  134 us (18%)
  other arithmetic  130 us (17%)
  matrix products  59.1 us (8%)
  starting transfers between devices  21.3 us (3%)
    slice x3, local copies, waits for them, and re-layouts, from_next(): inner = lax.slice_in_dim(field, 1, count, axis=axis)  131 us
    another operation x35, local copies, waits for them, and re-layouts, local_tiles(): return jnp.stack(tiles)  77.4 us
    convert_element_type x1, other arithmetic, local_tiles(): flux = (laplace_own(own) * cell_root).astype(jnp.bfloat16)  71.5 us
    all_gather x2, blocking collectives, body(): diag_all = lax.all_gather(diag_part, 'row', axis=2, tiled=True)  62 us
    all_gather x2, blocking collectives, body(): lax.all_gather(solved.reshape(width, row_blocks, 1, NB, n_sub).astype(jnp...  61.5 us
    dot_general x14, matrix products, contract_cells(): lax.dot_general(flat_left, flat_right, (((1,), (1,)), ((), ())), preferre...  58.3 us
    slice x2, local copies, waits for them, and re-layouts, local_tiles(): flux[:, :, :, -1]  47.3 us
    unnamed x16, local copies, waits for them, and re-layouts  41.7 us
  transfers between devices with their start and end apart: 6, of which 1 were waited for; matrix products, arithmetic and copies ran while one was open for 58% of the time, Pallas kernels for 0%

commit v1 on v0

--- a/solution.py
+++ b/solution.py
@@ -180,7 +180,7 @@
         part = local[first:last].reshape(PSUB, col_blocks, 1, NB, rows_here)
         whole = lax.all_gather(part, "col", axis=2, tiled=True).reshape(width, rows_here)
         diag_part = whole.reshape(width, row_blocks, 1, NB, n_sub)[:, :, :, :, first:last]
-        diag_all = lax.all_gather(diag_part, "row", axis=2, tiled=True)
+        diag_all = jnp.concatenate(lax.all_gather(diag_part, "row"), axis=2)
         diag = diag_all.transpose(0, 4, 1, 2, 3).reshape(width, width).T
         low = jnp.linalg.cholesky(diag)
         solved = lax.linalg.triangular_solve(low, whole, left_side=True, lower=True)

time: 749 us -> 755 us (level)
  transfers between devices with their start and end apart: 6 -> 6, of which waited for: 1 -> 1; matrix products, arithmetic and copies ran while one was open for 58% -> 57% of each run, Pallas kernels for 0% -> 0%
where the time goes in v1:
time: 755 us; the launch traced here: 744 us
  local copies, waits for them, and re-layouts  389 us (52%)
  blocking collectives  139 us (18%)
  other arithmetic  130 us (17%)
  matrix products  59.1 us (8%)
  starting transfers between devices  21.4 us (3%)
    slice x3, local copies, waits for them, and re-layouts, from_next(): inner = lax.slice_in_dim(field, 1, count, axis=axis)  131 us
    another operation x35, local copies, waits for them, and re-layouts, local_tiles(): return jnp.stack(tiles)  77.4 us
    convert_element_type x1, other arithmetic, local_tiles(): flux = (laplace_own(own) * cell_root).astype(jnp.bfloat16)  71.5 us
    all_gather x2, blocking collectives, body(): diag_all = jnp.concatenate(lax.all_gather(diag_part, 'row'), axis=2)  66.7 us
    all_gather x2, blocking collectives, body(): lax.all_gather(solved.reshape(width, row_blocks, 1, NB, n_sub).astype(jnp...  61.5 us
    dot_general x14, matrix products, contract_cells(): lax.dot_general(flat_left, flat_right, (((1,), (1,)), ((), ())), preferre...  58.2 us
    slice x2, local copies, waits for them, and re-layouts, local_tiles(): flux[:, :, :, -1]  47.3 us
    unnamed x16, local copies, waits for them, and re-layouts  41.7 us
  transfers between devices with their start and end apart: 6, of which 1 were waited for; matrix products, arithmetic and copies ran while one was open for 57% of the time, Pallas kernels for 0%

profile of v1, /device:TPU:0, one launch (start us, length us, event | category | flops | bytes accessed | tf_op | source)
XLA Modules:
  0.0 743.8 jit_solution(11160922071887930678)
XLA Ops:
  0.0 25.4 %fusion.90 = (bf16[32,32,64,1]{3,2,1,0:T(8,128)(2,1)}, bf16[32,32,64,1]{3,2,1,0:T(8,128)(2,1)}) fusion(bf16[32,32,64,128]{3,2,1,0:T(8,128)(2,1)} %param.10), kind=kLoop, calls=%fused_computation.170 | loop fusion | bytes 524288 | tf_op jit(solution)/shard_map/slice | solution.py:75
  25.4 19.4 %copy.551 = bf16[32,32,64,1]{1,0,2,3:T(8,128)(2,1)} copy(bf16[32,32,64,1]{3,2,1,0:T(8,128)(2,1)} %get-tuple-element.42) | data formatting | bytes 262144
  44.8 3.2 collective-permute-start.2
  48.0 19.4 %copy.552 = bf16[32,32,64,1]{1,0,2,3:T(8,128)(2,1)} copy(bf16[32,32,64,1]{3,2,1,0:T(8,128)(2,1)} %get-tuple-element.41) | data formatting | bytes 262144
  68.6 3.4 fusion.92
  74.8 5.5 collective-permute-start
  80.3 21.9 %copy_convert_fusion = f32[32,32,64,128]{3,0,1,2:T(8,128)} fusion(bf16[32,32,64,128]{3,2,1,0:T(8,128)(2,1)} %param.10), kind=kLoop, calls=%fused_computation.3 | loop fusion | flops 8388608 | bytes 50331648 | tf_op jit(solution)/shard_map/convert_element_type | solution.py:57
  102.2 45.9 %fusion.89 = (f32[32,32,64,127]{3,0,1,2:T(8,128)}, f32[32,32,64,127]{3,0,1,2:T(8,128)}) fusion(f32[32,32,64,128]{3,0,1,2:T(8,128)} %copy_convert_fusion), kind=kLoop, calls=%fused_computation.169 | loop fusion | bytes 133169152 | tf_op jit(solution)/shard_map/slice | solution.py:44
  148.1 44.0 %fusion.88 = (f32[32,32,63,128]{3,0,1,2:T(8,128)}, f32[32,32,63,128]{3,0,1,2:T(8,128)}) fusion(f32[32,32,64,128]{3,0,1,2:T(8,128)} %copy_convert_fusion), kind=kLoop, calls=%fused_computation.168 | loop fusion | bytes 132120576 | tf_op jit(solution)/shard_map/slice | solution.py:44
  192.1 41.5 %fusion.87 = (f32[32,31,64,128]{3,0,1,2:T(8,128)}, f32[32,31,64,128]{3,0,1,2:T(8,128)}) fusion(f32[32,32,64,128]{3,0,1,2:T(8,128)} %copy_convert_fusion), kind=kLoop, calls=%fused_computation.167 | loop fusion | bytes 130023424 | tf_op jit(solution)/shard_map/slice | solution.py:44
  234.2 3.3 select_add_fusion
  238.5 34.2 %fusion.8 = f32[32,32]{1,0:T(8,128)S(1)} fusion(bf16[32,32,64,128]{3,2,1,0:T(8,128)(2,1)} %param.10), kind=kOutput, calls=%fused_computation.18 | convolution fusion | flops 536870912 | bytes 16781312 | tf_op jit(solution)/shard_map/dot_general | solution.py:67
  273.4 71.5 %multiply_convert_fusion = bf16[32,32,64,128]{3,0,1,2:T(8,128)(2,1)} fusion(f32[32,32,64,127]{3,0,1,2:T(8,128)} %get-tuple-element.40, f32[32,32,64,127]{3,0,1,2:T(8,128)} %get-tuple-element.39, f32[32,32,63,128]{3,0,1,2:T(8,128)} %get-tuple-element.38, f32[32,32,63,128]{3,0,1,2:T(8,128)} %get-tuple-element.37, f32[32,31,64,128]{3,0,1,2:T(8,128)} %get-tuple-element.36, ...), kind=kLoop, calls=%fused_computation | loop fusion | flops 83886080 | bytes 232259584 | tf_op jit(solution)/shard_map/convert_element_type | solution.py:85
  344.9 25.9 %fusion.91 = (bf16[32,32,64,1]{3,0,1,2:T(8,128)(2,1)}, bf16[32,32,64,1]{3,0,1,2:T(8,128)(2,1)}) fusion(bf16[32,32,64,128]{3,0,1,2:T(8,128)(2,1)} %multiply_convert_fusion), kind=kLoop, calls=%fused_computation.171 | loop fusion | bytes 524288 | tf_op jit(solution)/shard_map/slice | solution.py:91
  370.8 13.5 %fusion.14 = f32[32,32]{1,0:T(8,128)} fusion(f32[32,32]{1,0:T(8,128)S(1)} %fusion.8, bf16[32,32,64,128]{3,0,1,2:T(8,128)(2,1)} %multiply_convert_fusion), kind=kOutput, calls=%fused_computation.20 | convolution fusion | flops 536871936 | bytes 16785408 | tf_op jit(solution)/shard_map/dot_general | solution.py:67
  385.6 21.2 %copy.391 = bf16[32,32,64,1]{2,1,0,3:T(8,128)(2,1)S(1)} copy(bf16[32,32,64,1]{3,0,1,2:T(8,128)(2,1)} %get-tuple-element.44) | data formatting | bytes 262144 | tf_op jit(solution)/shard_map/slice | solution.py:90
  407.5 21.4 %copy.399 = bf16[32,32,64,1]{2,1,0,3:T(8,128)(2,1)S(1)} copy(bf16[32,32,64,1]{3,0,1,2:T(8,128)(2,1)} %get-tuple-element.43) | data formatting | bytes 262144 | tf_op jit(solution)/shard_map/slice | solution.py:91
  430.7 3.1 copy.414
  441.6 3.1 copy.421
  444.9 3.4 copy.422
  451.9 3.4 copy.425
  464.4 3.9 copy.418
  468.5 4.2 copy.419
  475.2 3.9 copy.415
  479.3 4.2 copy.416
  490.5 3.2 copy.407
  494.9 3.9 copy.427
  498.9 4.2 copy.428
  504.3 4.0 copy.429
  508.5 4.1 copy.430
  516.0 3.9 copy.431
  520.1 4.1 copy.432
  526.6 3.9 copy.433
  530.7 4.2 copy.434
  534.9 7.7 %stack.75 = f32[21,2,8,2,4,4,2]{0,2,6,5,4,3,1:T(8,128)} concatenate(f32[1,2,8,2,4,4,2]{0,2,6,5,4,3,1:T(8,128)S(1)} %copy.414, f32[1,2,8,2,4,4,2]{0,2,6,5,4,3,1:T(8,128)} %copy.415, f32[1,2,8,2,4,4,2]{0,2,6,5,4,3,1:T(8,128)} %copy.416, f32[1,2,8,2,4,4,2]{0,2,6,5,4,3,1:T(8,128)} %copy.417, f32[1,2,8,2,4,4,2]{0,2,6,5,4,3,1:T(8,128)} %copy.418, f32[1,2,8,2,4,4,2]{0,2,6,5,4,3,1:T(8,128)} %copy.419, ...), dimensions={0} | concatenate | bytes 172032 | tf_op jit(solution)/shard_map/stack | solution.py:108
  546.5 5.5 all-to-all-start
  563.8 4.5 all-to-all-start.1
  568.3 4.3 all-to-all-done.1
  575.7 5.2 all_gather.24
  581.0 33.8 %all-gather = f32[512,2,1,2,2]{4,3,2,1,0:T(2,128)S(1)} all-gather(f32[64,2,1,2,2]{4,3,2,1,0:T(2,128)S(1)} %slice_bitcast_fusion.5), channel_id=2, replica_groups=mesh['row'=8,'col'=4] {'row'}, dimensions={0}, use_global_device_ids=true | all-gather | bytes 18432 | tf_op jit(solution)/shard_map/all_gather | solution.py:183
  615.7 5.8 cholesky.44
  622.9 4.9 custom-call.6
  628.2 30.8 %all_gather.27 = bf16[64,2,8,2,32]{0,4,3,1,2:T(8,128)(2,1)S(1)} all-gather(bf16[64,2,1,2,32]{0,4,3,1,2:T(8,128)(2,1)S(1)} %bitcast.349), channel_id=1, replica_groups=mesh['row'=8,'col'=4] {'row'}, dimensions={2}, use_global_device_ids=true | all-gather | bytes 147456 | tf_op jit(solution)/shard_map/all_gather | solution.py:192
  659.4 5.2 all_gather.28
  664.9 32.9 %all-gather.1 = f32[512,2,1,2,2]{4,3,2,1,0:T(2,128)S(1)} all-gather(f32[64,2,1,2,2]{4,3,2,1,0:T(2,128)S(1)} %slice_bitcast_fusion.4), channel_id=3, replica_groups=mesh['row'=8,'col'=4] {'row'}, dimensions={0}, use_global_device_ids=true | all-gather | bytes 18432 | tf_op jit(solution)/shard_map/all_gather | solution.py:183
  698.8 5.8 cholesky.55
  706.0 4.9 custom-call.7
  711.2 30.7 %all_gather.31 = bf16[64,2,8,2,32]{0,4,3,1,2:T(8,128)(2,1)S(1)} all-gather(bf16[64,2,1,2,32]{0,4,3,1,2:T(8,128)(2,1)S(1)} %bitcast.351), channel_id=1, replica_groups=mesh['row'=8,'col'=4] {'row'}, dimensions={2}, use_global_device_ids=true | all-gather | bytes 147456 | tf_op jit(solution)/shard_map/all_gather | solution.py:192
  (194 shorter events, 75.3 us)
Async XLA Ops:
  44.8 389.9 %collective-permute-start.2 = (bf16[32,32,1,64]{1,0,3,2:T(8,128)(2,1)}, bf16[32,32,1,64]{1,0,3,2:T(8,128)(2,1)}, u32[]{:S(2)}, u32[]{:S(2)}) collective-permute-start(bf16[32,32,1,64]{1,0,3,2:T(8,128)(2,1)} %bitcast.32), channel_id=1, source_target_pairs={{0,1},{1,2},{2,3},{4,5},{5,6},{6,7},{8,9},{9,10},{10,11},{12,13},{... | collective-permute-start | bytes 393224 | tf_op jit(solution)/shard_map/ppermute | solution.py:19
  67.3 369.4 %collective-permute-start.3 = (bf16[32,32,1,64]{1,0,3,2:T(8,128)(2,1)}, bf16[32,32,1,64]{1,0,3,2:T(8,128)(2,1)}, u32[]{:S(2)}, u32[]{:S(2)}) collective-permute-start(bf16[32,32,1,64]{1,0,3,2:T(8,128)(2,1)} %bitcast.43), channel_id=1, source_target_pairs={{1,0},{2,1},{3,2},{5,4},{6,5},{7,6},{9,8},{10,9},{11,10},{13,12},{... | collective-permute-start | bytes 393224 | tf_op jit(solution)/shard_map/ppermute | solution.py:21
  72.7 389.1 %collective-permute-start.1 = (bf16[32,32,1,128]{3,1,0,2:T(8,128)(2,1)}, bf16[32,32,1,128]{3,1,0,2:T(8,128)(2,1)}, u32[]{:S(2)}, u32[]{:S(2)}) collective-permute-start(bf16[32,32,1,128]{3,1,0,2:T(8,128)(2,1)} %copy.550), channel_id=1, source_target_pairs={{4,0},{8,4},{12,8},{16,12},{20,16},{24,20},{28,24},{5,1},{9,5},{13... | collective-permute-start | bytes 786440 | tf_op jit(solution)/shard_map/ppermute | solution.py:21
  74.8 397.9 %collective-permute-start = (bf16[32,32,1,128]{3,1,2,0:T(8,128)(2,1)}, bf16[32,32,1,128]{3,1,2,0:T(8,128)(2,1)}, u32[]{:S(2)}, u32[]{:S(2)}) collective-permute-start(bf16[32,32,1,128]{3,1,2,0:T(8,128)(2,1)} %copy.549), channel_id=1, source_target_pairs={{0,4},{4,8},{8,12},{12,16},{16,20},{20,24},{24,28},{1,5},{5,9},{9,... | collective-permute-start | bytes 786440 | tf_op jit(solution)/shard_map/ppermute | solution.py:19
  192.1 41.5 %copy-start.4 = (f32[4]{0:T(128)S(1)}, f32[4]{0:T(128)}, u32[]{:S(2)}) copy-start(f32[4]{0:T(128)} %param.12) | copy-start | bytes 52
  192.1 42.2 %copy-start = (s32[32,64,128]{2,1,0:T(8,128)S(1)}, s32[32,64,128]{2,1,0:T(8,128)}, u32[]{:S(2)}) copy-start(s32[32,64,128]{2,1,0:T(8,128)} %param.11) | copy-start | bytes 3145732
  440.2 85.3 %copy-start.1 = (f32[32]{0:T(128)S(1)}, f32[32]{0:T(128)}, u32[]{:S(2)}) copy-start(f32[32]{0:T(128)} %get-tuple-element.31) | copy-start | bytes 388
  444.9 182.9 %copy-start.3 = (pred[128]{0:T(512)(128)(4,1)S(1)}, pred[128]{0:T(512)(128)(4,1)}, u32[]{:S(2)}) copy-start(pred[128]{0:T(512)(128)(4,1)} %broadcast_compare_fusion.3) | copy-start | bytes 388
  455.3 203.9 %copy-start.2 = (pred[32]{0:T(512)(128)(4,1)S(1)}, pred[32]{0:T(512)(128)(4,1)}, u32[]{:S(2)}) copy-start(pred[32]{0:T(512)(128)(4,1)} %iota_compare_fusion.2) | copy-start | bytes 100
  546.5 16.6 %all-to-all-start = ((f32[8,4,672]{2,1,0:T(4,128)}), f32[8,4,672]{2,1,0:T(4,128)S(1)}, u32[]{:S(2)}, u32[]{:S(2)}) async-start(f32[8,4,672]{2,1,0:T(4,128)} %copy.436), calls=%async_computation | async-start | bytes 196608 | tf_op jit(solution)/shard_map/all_to_all | solution.py:160
  563.8 8.8 %all-to-all-start.1 = ((f32[8,4,672]{2,0,1:T(8,128)}), f32[8,4,672]{2,0,1:T(8,128)S(1)}, u32[]{:S(2)}, u32[]{:S(2)}) async-start(f32[8,4,672]{2,0,1:T(8,128)} %copy.437), calls=%async_computation.1 | async-start | bytes 196608 | tf_op jit(solution)/shard_map/all_to_all | solution.py:159
